TPU v7x, 32 devices: a whole 2x2x4 slice. The times are simulated.
32 devices in a mesh: fsdp: 8 (over y, x, core), rep: 4 (over z).
Axes of the slice: x: 2, y: 2, z: 4, core: 2. Of those that a mesh axis runs over, the one named last changes fastest.
Arguments:
- tokens: bfloat16 [65536, 768], P(('fsdp', 'rep')), may hold values from -6 to 6
- segment_ids: int32 [65536], P(('fsdp', 'rep')), may hold values from -1 to 8, as said below
- cotangent: bfloat16 [65536, 768], P(('fsdp', 'rep')), may hold values from -8 to 8
- norm_params: bfloat16 [4, 768], P(None, 'fsdp')
- qkv_weight: bfloat16 [768, 2304], P(None, 'fsdp'), may hold values from -0.21875 to 0.21875
- proj_weight: bfloat16 [768, 768], P(None, 'fsdp'), may hold values from -1.25 to 1.25
- up_weight: bfloat16 [768, 3072], P(None, 'fsdp'), may hold values from -0.21875 to 0.21875
- down_weight: bfloat16 [3072, 768], P(None, 'fsdp'), may hold values from -0.109375 to 0.109375
- target_norms: float32 [4, 768], P(None, 'fsdp'), may hold values from -3 to 3
- target_qkv: float32 [768, 2304], P(None, 'fsdp'), may hold values from -0.21875 to 0.21875
- target_proj: float32 [768, 768], P(None, 'fsdp'), may hold values from -1.25 to 1.25
- target_up: float32 [768, 3072], P(None, 'fsdp'), may hold values from -0.21875 to 0.21875
- target_down: float32 [3072, 768], P(None, 'fsdp'), may hold values from -0.109375 to 0.109375
Outputs:
- block_output: bfloat16 [65536, 768], P(('fsdp', 'rep'))
- input_grad: bfloat16 [65536, 768], P(('fsdp', 'rep'))
- norm_grad: float32 [4, 768], P(None, 'fsdp')
- qkv_grad: float32 [768, 2304], P(None, 'fsdp')
- proj_grad: float32 [768, 768], P(None, 'fsdp')
- up_grad: float32 [768, 3072], P(None, 'fsdp')
- down_grad: float32 [3072, 768], P(None, 'fsdp')
- new_target_norms: float32 [4, 768], P(None, 'fsdp')
- new_target_qkv: float32 [768, 2304], P(None, 'fsdp')
- new_target_proj: float32 [768, 768], P(None, 'fsdp')
- new_target_up: float32 [768, 3072], P(None, 'fsdp')
- new_target_down: float32 [3072, 768], P(None, 'fsdp')
Inputs may be any that keep to these rules, and one draw needn't show every extreme that they name: `segment_ids`: in each packed row of 1024 slots, images fill consecutive slots from the row's start with ids 0, 1, 2, ... in order; each image has 98 to 196 slots and one image of each row has exactly 196; the remaining slots at the row's end are -1. In the first packed row all images except the one of 196 slots have exactly 98 slots.
All inputs are finite; a program needn't handle non-finite values.
Results may differ from a plain program's by a relative error of at most 0.014.
Values may be sent and summed in bfloat16 or wider, within the bound.
No kernel may reach another device: no remote copies, remote signals or barrier semaphores. Data moves between devices by JAX's collectives and lax.ppermute only.
A program may use at most 256 MiB of HBM per device.

v0:
```python
import jax
import jax.numpy as jnp
from jax import lax
from jax.sharding import PartitionSpec as P

HEAD = 64
ROW_LEN = 1024
layer_eps = 1e-06
ema_rate = 0.75


def layer_norm(values, gain, shift):
    center = values - jnp.mean(values, axis=-1, keepdims=True)
    spread = jnp.mean(center * center, axis=-1, keepdims=True)
    return center * lax.rsqrt(spread + layer_eps) * gain + shift


def gelu_exact(values):
    return jax.nn.gelu(values, approximate=False)


def product(left, right):
    return jnp.dot(left, right, preferred_element_type=jnp.float32)


def outer_sum(left, right):
    return lax.dot_general(
        left, right, (((0,), (0,)), ((), ())), preferred_element_type=jnp.float32
    )


def against(left, right):
    return lax.dot_general(
        left, right, (((1,), (1,)), ((), ())), preferred_element_type=jnp.float32
    )


def split_heads(matrix, rows):
    count, width = matrix.shape
    heads = width // HEAD
    shaped = matrix.reshape(rows, count // rows, heads, HEAD)
    return shaped.transpose(0, 2, 1, 3).reshape(rows * heads, count // rows, HEAD)


def merge_heads(stacked, rows):
    items, length, size = stacked.shape
    heads = items // rows
    shaped = stacked.reshape(rows, heads, length, size).transpose(0, 2, 1, 3)
    return shaped.reshape(rows * length, heads * size)


def masked_scores(query, keyset, segment):
    same = segment[:, None] == segment[None, :]
    return jnp.where(same, against(query, keyset) * 0.125, -1e30)


def head_forward(item):
    query, keyset, value, segment = item
    scores = masked_scores(query, keyset, segment)
    top = jnp.max(scores, axis=1, keepdims=True)
    expo = jnp.exp(scores - top)
    total = jnp.sum(expo, axis=1, keepdims=True)
    weights = (expo / total).astype(jnp.bfloat16)
    return (product(weights, value), top, total)


def head_backward(item):
    query, keyset, value, segment, top, total, grad_head = item
    scores = masked_scores(query, keyset, segment)
    probs = jnp.exp(scores - top) / total
    grad_probs = against(grad_head, value)
    center = jnp.sum(probs * grad_probs, axis=1, keepdims=True)
    grad_scores = (probs * (grad_probs - center)).astype(jnp.bfloat16)
    grad_query = product(grad_scores, keyset) * 0.125
    grad_key = outer_sum(grad_scores, query) * 0.125
    grad_value = outer_sum(probs.astype(jnp.bfloat16), grad_head)
    return (grad_query, grad_key, grad_value)


def per_device(
    tokens,
    segment_ids,
    cotangent,
    norm_params,
    qkv_weight,
    proj_weight,
    up_weight,
    down_weight,
    target_norms,
    target_qkv,
    target_proj,
    target_up,
    target_down,
):
    norms, w_qkv, w_proj, w_up, w_down = (
        lax.all_gather(norm_params, "fsdp", axis=1, tiled=True),
        lax.all_gather(qkv_weight, "fsdp", axis=1, tiled=True),
        lax.all_gather(proj_weight, "fsdp", axis=1, tiled=True),
        lax.all_gather(up_weight, "fsdp", axis=1, tiled=True),
        lax.all_gather(down_weight, "fsdp", axis=1, tiled=True),
    )
    gains = norms.astype(jnp.float32)
    count, width = tokens.shape
    rows = count // ROW_LEN
    heads = width // HEAD
    inputs = tokens.astype(jnp.float32)
    valid = (segment_ids >= 0).astype(jnp.float32)[:, None]
    first = layer_norm(inputs, gains[0], gains[1]).astype(jnp.bfloat16)
    qkv = product(first, w_qkv).astype(jnp.bfloat16)
    query = split_heads(qkv[:, :width], rows)
    keyset = split_heads(qkv[:, width : 2 * width], rows)
    value = split_heads(qkv[:, 2 * width :], rows)
    segments = jnp.repeat(segment_ids.reshape(rows, ROW_LEN), heads, axis=0)
    head_out, tops, totals = lax.map(head_forward, (query, keyset, value, segments))
    attended = merge_heads(head_out, rows).astype(jnp.bfloat16)
    middle = inputs + product(attended, w_proj)
    second = layer_norm(middle, gains[2], gains[3]).astype(jnp.bfloat16)
    upper = product(second, w_up)
    activated = gelu_exact(upper).astype(jnp.bfloat16)
    final = middle + product(activated, w_down)
    block_output = (final * valid).astype(jnp.bfloat16)
    norms, w_qkv, w_proj, w_up, w_down = (
        lax.all_gather(norm_params, "fsdp", axis=1, tiled=True),
        lax.all_gather(qkv_weight, "fsdp", axis=1, tiled=True),
        lax.all_gather(proj_weight, "fsdp", axis=1, tiled=True),
        lax.all_gather(up_weight, "fsdp", axis=1, tiled=True),
        lax.all_gather(down_weight, "fsdp", axis=1, tiled=True),
    )
    gains = norms.astype(jnp.float32)
    grad_out = (cotangent.astype(jnp.float32) * valid).astype(jnp.bfloat16)
    grad_down = outer_sum(activated, grad_out)
    grad_act = against(grad_out, w_down)
    gelu_back = jax.vjp(gelu_exact, upper)[1]
    grad_upper = gelu_back(grad_act)[0].astype(jnp.bfloat16)
    grad_up = outer_sum(second, grad_upper)
    grad_second = against(grad_upper, w_up)
    second_back = jax.vjp(layer_norm, middle, gains[2], gains[3])[1]
    grad_mid_norm, grad_gain_two, grad_shift_two = second_back(grad_second)
    grad_middle = grad_out.astype(jnp.float32) + grad_mid_norm
    grad_branch = grad_middle.astype(jnp.bfloat16)
    grad_proj = outer_sum(attended, grad_branch)
    grad_attended = against(grad_branch, w_proj).astype(jnp.bfloat16)
    grad_heads = split_heads(grad_attended, rows)
    grad_query, grad_key, grad_value = lax.map(
        head_backward, (query, keyset, value, segments, tops, totals, grad_heads)
    )
    grad_qkv = jnp.concatenate(
        [merge_heads(grad_query, rows), merge_heads(grad_key, rows), merge_heads(grad_value, rows)],
        axis=1,
    ).astype(jnp.bfloat16)
    grad_wqkv = outer_sum(first, grad_qkv)
    grad_first = against(grad_qkv, w_qkv)
    first_back = jax.vjp(layer_norm, inputs, gains[0], gains[1])[1]
    grad_in_norm, grad_gain_one, grad_shift_one = first_back(grad_first)
    input_grad = (grad_middle + grad_in_norm).astype(jnp.bfloat16)
    grad_norms = jnp.stack([grad_gain_one, grad_shift_one, grad_gain_two, grad_shift_two])
    owned = (
        lax.psum_scatter(grad_norms, "fsdp", scatter_dimension=1, tiled=True),
        lax.psum_scatter(grad_wqkv, "fsdp", scatter_dimension=1, tiled=True),
        lax.psum_scatter(grad_proj, "fsdp", scatter_dimension=1, tiled=True),
        lax.psum_scatter(grad_up, "fsdp", scatter_dimension=1, tiled=True),
        lax.psum_scatter(grad_down, "fsdp", scatter_dimension=1, tiled=True),
    )
    summed = (
        lax.psum(owned[0].astype(jnp.bfloat16), "rep").astype(jnp.float32),
        lax.psum(owned[1].astype(jnp.bfloat16), "rep").astype(jnp.float32),
        lax.psum(owned[2].astype(jnp.bfloat16), "rep").astype(jnp.float32),
        lax.psum(owned[3].astype(jnp.bfloat16), "rep").astype(jnp.float32),
        lax.psum(owned[4].astype(jnp.bfloat16), "rep").astype(jnp.float32),
    )
    keep_rate = 1.0 - ema_rate
    new_norms = ema_rate * target_norms + keep_rate * norm_params.astype(jnp.float32)
    new_qkv = ema_rate * target_qkv + keep_rate * qkv_weight.astype(jnp.float32)
    new_proj = ema_rate * target_proj + keep_rate * proj_weight.astype(jnp.float32)
    new_up = ema_rate * target_up + keep_rate * up_weight.astype(jnp.float32)
    new_down = ema_rate * target_down + keep_rate * down_weight.astype(jnp.float32)
    return (
        block_output,
        input_grad,
        summed[0],
        summed[1],
        summed[2],
        summed[3],
        summed[4],
        new_norms,
        new_qkv,
        new_proj,
        new_up,
        new_down,
    )


def solution(mesh):
    return jax.shard_map(
        per_device,
        mesh=mesh,
        in_specs=(
            P(("fsdp", "rep"), None),
            P(("fsdp", "rep")),
            P(("fsdp", "rep"), None),
            P(None, "fsdp"),
            P(None, "fsdp"),
            P(None, "fsdp"),
            P(None, "fsdp"),
            P(None, "fsdp"),
            P(None, "fsdp"),
            P(None, "fsdp"),
            P(None, "fsdp"),
            P(None, "fsdp"),
            P(None, "fsdp"),
        ),
        out_specs=(
            P(("fsdp", "rep"), None),
            P(("fsdp", "rep"), None),
            P(None, "fsdp"),
            P(None, "fsdp"),
            P(None, "fsdp"),
            P(None, "fsdp"),
            P(None, "fsdp"),
            P(None, "fsdp"),
            P(None, "fsdp"),
            P(None, "fsdp"),
            P(None, "fsdp"),
            P(None, "fsdp"),
        ),
        check_vma=False,
    )
```

profile of v0, /device:TPU:0, one launch (start us, length us, event | category | flops | bytes accessed | tf_op | source)
XLA Modules:
  0.0 1168.2 jit_solution(18009675124772495406)
XLA Ops:
  12.0 3.2 copy.114
  16.7 10.4 all-gather
  27.2 4.7 copy.127
  32.0 14.6 %all-gather.6.cloned.1.call-done = bf16[768,2304]{0,1:T(8,128)(2,1)} async-done(((bf16[768,288]{0,1:T(8,128)(2,1)}), bf16[768,2304]{0,1:T(8,128)(2,1)}) %all-gather.6.cloned.1.call-update) | async-done | bytes 3538960 | tf_op jit(solution)/shard_map/all_gather | solution.py:97
  46.6 10.6 convolution_convert_fusion
  57.3 3.8 fusion.77
  61.1 4.8 copy.116
  65.9 6.1 reshape.164
  72.0 9.8 copy.144
  81.8 4.8 copy.118
  86.6 6.1 reshape.166
  92.7 9.9 copy.145
  102.7 4.6 copy.120
  107.3 6.1 reshape.168
  113.4 9.7 copy.146
  125.2 152.9 %while.28 = (s32[]{:T(128)}, bf16[24,1024,64]{1,2,0:T(8,128)(2,1)}, f32[24,1024,1]{1,2,0:T(1,128)}, f32[24,1024,1]{1,2,0:T(1,128)}, s32[24,1024]{1,0:T(8,128)S(1...) while((s32[]{:T(128)}, bf16[24,1024,64]{1,2,0:T(8,128)(2,1)}, ...), condition=%wide.region_5.6_spmd, body=%wide.region_2.5_spmd.sunk | while | flops 284162048 | bytes 13699681 | solution.py:114
  278.2 5.2 copy.125
  286.1 4.9 fusion.78
  296.4 67.5 %multiply_convert_fusion.1 = (bf16[2048,3072]{1,0:T(8,128)(2,1)}, f32[2048,3072]{1,0:T(8,128)}, f32[2048,3072]{1,0:T(8,128)}) fusion(bf16[768,3072]{1,0:T(8,128)(2,1)} %all-gather.10.cloned.1.call-done, bf16[2048,768]{0,1:T(8,128)(2,1)} %add_convert_fusion.4.clone.4), kind=kOutput, calls=%fused_computation.61 | convolution fusion | flops 10072621056 | bytes 70778880 | tf_op jit(solution)/shard_map/dot_general | solution.py:23
  364.0 27.9 %add_convert_fusion = bf16[2048,3072]{1,0:T(8,128)(2,1)} fusion(f32[2048,3072]{1,0:T(8,128)} %get-tuple-element.291, f32[2048,3072]{1,0:T(8,128)} %get-tuple-element.305, bf16[3072,768]{0,1:T(8,128)(2,1)} %all-gather.12.cloned.1.call-done, bf16[2048,768]{0,1:T(8,128)(2,1)S(1)} %copy-done.6, f32[2048]{0:T(1024)S(1)} %copy-done.21), kind=kOutput, calls=%fused_computation.60 | convolution fusion | flops 9756475392 | bytes 70787072 | tf_op jit(solution)/shard_map/dot_general | solution.py:33
  391.9 16.6 %fusion.79 = (f32[768]{0:T(1024)}, f32[2048,768]{1,0:T(8,128)}) fusion(bf16[2048,3072]{1,0:T(8,128)(2,1)} %add_convert_fusion, bf16[768,3072]{1,0:T(8,128)(2,1)} %all-gather.10.cloned.1.call-done), kind=kOutput, calls=%fused_computation.135 | convolution fusion | flops 9665248256 | bytes 23596032 | tf_op jit(solution)/shard_map/dot_general | solution.py:33
  408.4 6.7 copy.128
  415.2 6.7 multiply_reduce_fusion.1
  429.3 4.0 fusion.81
  433.3 5.3 convolution_convert_fusion.1
  438.6 3.2 copy.129
  441.8 3.9 reshape.170
  445.7 9.8 copy.149
  460.1 320.7 %while.29 = (s32[]{:T(128)}, bf16[24,1024,64]{1,2,0:T(8,128)(2,1)S(1)}, bf16[24,1024,64]{1,2,0:T(8,128)(2,1)}, bf16[24,1024,64]{1,2,0:T(8,128)(2,1)}, s32[24,102...) while((s32[]{:T(128)}, ...), condition=%wide.region_12.13_spmd, body=%wide.region_10.12_spmd.sunk | while | flops 682753024 | bytes 34133116 | solution.py:144
  780.8 3.2 copy.135
  785.1 3.2 copy.136
  789.4 5.3 copy.137
  796.9 3.7 copy-done.12
  800.6 10.0 fusion.70
  811.4 17.0 %fusion.73 = f32[768,3072]{1,0:T(8,128)} fusion(bf16[2048,3072]{1,0:T(8,128)(2,1)} %add_convert_fusion, f32[2048,768]{0,1:T(8,128)} %copy-done.2, f32[768]{0:T(1024)S(1)} %copy-done.35, f32[768]{0:T(1024)S(1)} %copy-done.33, f32[2048]{0:T(1024)S(1)} %copy-done.20, f32[2048]{0:T(1024)S(1)} %copy-done.15), kind=kOutput, calls=%fused_computation.130 | convolution fusion | flops 9671540736 | bytes 28334080 | tf_op jit(solution)/shard_map/dot_general | solution.py:27
  828.5 16.1 %fusion.66 = f32[3072,768]{0,1:T(8,128)} fusion(bf16[2048,3072]{1,0:T(8,128)(2,1)} %get-tuple-element.290, bf16[2048,768]{0,1:T(8,128)(2,1)} %copy.127, f32[2048]{0:T(1024)S(1)} %copy-done.21), kind=kOutput, calls=%fused_computation.102 | convolution fusion | flops 9668395008 | bytes 25174016 | tf_op jit(solution)/shard_map/dot_general | solution.py:27
  854.1 12.1 %fusion.80 = (f32[768]{0:T(1024)S(1)}, f32[2048,768]{1,0:T(8,128)}) fusion(bf16[2048,2304]{0,1:T(8,128)(2,1)} %copy-done.12, bf16[768,2304]{0,1:T(8,128)(2,1)S(1)} %copy-done.43), kind=kOutput, calls=%fused_computation.136 | convolution fusion | flops 7249329152 | bytes 19270656 | tf_op jit(solution)/shard_map/dot_general | solution.py:33
  866.1 6.6 copy.138
  872.7 4.1 fusion.64
  877.5 3.1 fusion.62
  882.0 10.0 add_convert_fusion.1
  892.1 4.9 copy.142
  900.6 55.7 %reduce-scatter.12.cloned.1.call-done = f32[768,384]{1,0:T(8,128)} async-done(((f32[768,3072]{1,0:T(8,128)}), f32[768,384]{1,0:T(8,128)}) %reduce-scatter.12.cloned.1.call-update) | async-done | bytes 1179664 | tf_op jit(solution)/shard_map/reduce_scatter | solution.py:161
  958.5 77.9 %reduce-scatter.14.cloned.1.call-done = f32[3072,96]{0,1:T(8,128)} async-done(((f32[3072,768]{0,1:T(8,128)}), f32[3072,96]{0,1:T(8,128)}) %reduce-scatter.14.cloned.1.call-update) | async-done | bytes 1179664 | tf_op jit(solution)/shard_map/reduce_scatter | solution.py:162
  1038.5 17.1 %multiply_convert_fusion.3 = bf16[2048,768]{0,1:T(8,128)(2,1)S(1)} fusion(f32[2048,768]{0,1:T(8,128)} %copy-done.2, bf16[2048,3072]{1,0:T(8,128)(2,1)} %get-tuple-element.290, bf16[3072,768]{0,1:T(8,128)(2,1)} %all-gather.12.cloned.1.call-done, f32[2048]{0:T(1024)S(1)} %copy-done.21), kind=kOutput, calls=%fused_computation.97 | convolution fusion | flops 9668395008 | bytes 26746880 | tf_op jit(solution)/shard_map/dot_general | solution.py:23
  1058.4 14.9 %reduce-scatter.16.cloned.1.call-done = f32[96,4]{1,0:T(8,128)} async-done(((f32[768,4]{1,0:T(8,128)}), f32[96,4]{1,0:T(8,128)}) %reduce-scatter.16.cloned.1.call-update) | async-done | bytes 1552
  1074.2 11.8 %psum.35 = bf16[4,96]{1,0:T(4,128)(2,1)S(1)} all-reduce(bf16[4,96]{1,0:T(4,128)(2,1)S(1)} %copy.152), channel_id=1, replica_groups=mesh['fsdp'=8,'rep'=4] {'rep'}, use_global_device_ids=true, to_apply=%region_20.21 | all-reduce | flops 384 | bytes 1536 | tf_op jit(solution)/shard_map/psum | solution.py:165
  1086.5 66.5 %all-reduce.3.cloned.1.call-done = (bf16[768,288]{0,1:T(8,128)(2,1)}, bf16[768,96]{0,1:T(8,128)(2,1)}, bf16[768,384]{1,0:T(8,128)(2,1)}, bf16[3072,96]{0,1:T(8,128)(2,1)}) async-done(((bf16[768,288]{0,1:T(8,128)(2,1)}, bf16[768,96]{0,1:T(8,128)(2,1)}, bf16[768,384]{1,0:T(8,128)(2,1)}, bf16[3072,96]{0,1:T(8,128)(2,1)}), (bf16[768,288]{0,1:T(8,128)(2,1)}, bf16[768,96]{0,1:T(8,128)(2,1)}, ...) | async-done | bytes 1769488 | tf_op jit(solution)/shard_map/psum | solution.py:166
  (485 shorter events, 537.1 us)
Async XLA Ops:
  7.2 39.4 %all-gather.6.cloned.1.call-start = ((), (), s32[]{:S(2)}) async-start(), calls=%async_computation.5 | async-start | bytes 3981312 | tf_op jit(solution)/shard_map/all_gather | solution.py:97
  7.9 278.2 %all-gather.8.cloned.1.call-start = ((), (), s32[]{:S(2)}) async-start(), calls=%async_computation.6 | async-start | bytes 1327104 | tf_op jit(solution)/shard_map/all_gather | solution.py:98
  8.7 287.7 %all-gather.10.cloned.1.call-start = ((), (), s32[]{:S(2)}) async-start(), calls=%async_computation.7 | async-start | bytes 5308416 | tf_op jit(solution)/shard_map/all_gather | solution.py:99
  9.4 354.5 %all-gather.12.cloned.1.call-start = ((), (), s32[]{:S(2)}) async-start(), calls=%async_computation.8 | async-start | bytes 5308416 | tf_op jit(solution)/shard_map/all_gather | solution.py:100
  10.0 887.0 %reduce-scatter.10.cloned.1.call-start = ((), (), s32[]{:S(2)}) async-start(), calls=%async_computation.10 | async-start | bytes 2654208 | tf_op jit(solution)/shard_map/reduce_scatter | solution.py:160
  12.0 4.6 copy-start.39
  15.2 270.8 %copy-start = (bf16[2048,768]{0,1:T(8,128)(2,1)}, bf16[2048,768]{0,1:T(8,128)(2,1)S(1)}, u32[]{:S(2)}) copy-start(bf16[2048,768]{0,1:T(8,128)(2,1)S(1)} %copy.114) | copy-start | bytes 9437188
  15.8 41.5 %copy-start.16 = (f32[2048]{0:T(1024)}, f32[2048]{0:T(1024)S(1)}, u32[]{:S(2)}) copy-start(f32[2048]{0:T(1024)S(1)} %broadcast_multiply_fusion.1) | copy-start | bytes 24580
  16.6 10.5 copy-start.24
  16.6 40.6 %copy-start.28 = (f32[2048]{0:T(1024)}, f32[2048]{0:T(1024)S(1)}, u32[]{:S(2)}) copy-start(f32[2048]{0:T(1024)S(1)} %fusion.68) | copy-start | bytes 24580
  27.2 30.1 %copy-start.30 = (f32[768]{0:T(1024)}, f32[768]{0:T(1024)S(1)}, u32[]{:S(2)}) copy-start(f32[768]{0:T(1024)S(1)} %get-tuple-element.245) | copy-start | bytes 9220
  27.2 30.1 %copy-start.37 = (f32[768]{0:T(1024)}, f32[768]{0:T(1024)S(1)}, u32[]{:S(2)}) copy-start(f32[768]{0:T(1024)S(1)} %get-tuple-element.244) | copy-start | bytes 9220
  27.2 265.6 %copy-start.32 = (f32[768]{0:T(1024)}, f32[768]{0:T(1024)S(1)}, u32[]{:S(2)}) copy-start(f32[768]{0:T(1024)S(1)} %get-tuple-element.242) | copy-start | bytes 9220
  27.2 265.6 %copy-start.34 = (f32[768]{0:T(1024)}, f32[768]{0:T(1024)S(1)}, u32[]{:S(2)}) copy-start(f32[768]{0:T(1024)S(1)} %get-tuple-element.243) | copy-start | bytes 9220
  278.2 7.9 copy-start.18
  291.0 2.8 copy-start.2
  296.4 67.5 %copy-start.6 = (bf16[2048,768]{0,1:T(8,128)(2,1)S(1)}, bf16[2048,768]{0,1:T(8,128)(2,1)}, u32[]{:S(2)}) copy-start(bf16[2048,768]{0,1:T(8,128)(2,1)} %copy.127) | copy-start | bytes 9437188
  296.4 67.5 %copy-start.21 = (f32[2048]{0:T(1024)S(1)}, f32[2048]{0:T(1024)}, u32[]{:S(2)}) copy-start(f32[2048]{0:T(1024)} %compare_convert_fusion) | copy-start | bytes 24580
  408.4 6.7 copy-start.15
  408.4 6.7 copy-start.20
  408.4 6.7 copy-start.33
  408.4 13.5 %slice-start = ((s8[6291456]{0:T(1024)(128)(4,1)}), s8[2097152]{0:T(1024)(128)(4,1)S(1)}, s32[]{:S(2)}) async-start(s8[6291456]{0:T(1024)(128)(4,1)} %bitcast.182), calls=%async_computation.15 | async-start | bytes 4194304
  415.2 6.8 copy-start.27
  415.2 6.8 slice-start.1
  415.2 7.7 copy-start.4
  425.1 3.2 copy-start.5
  425.1 3.2 copy-start.22
  425.2 4.1 copy-start.9
  455.5 443.1 %reduce-scatter.8.cloned.1.call-start = ((), (), s32[]{:S(2)}) async-start(), calls=%async_computation.9 | async-start | bytes 7962624 | tf_op jit(solution)/shard_map/reduce_scatter | solution.py:159
  780.8 4.3 copy-start.8
  796.1 4.5 copy-start.1
  796.1 4.5 copy-start.17
  796.1 4.5 copy-start.29
  796.1 4.5 copy-start.31
  796.1 4.5 copy-start.38
  796.9 3.7 copy-start.12
  810.7 145.6 %reduce-scatter.12.cloned.1.call-start = ((), (), s32[]{:S(2)}) async-start(), calls=%async_computation.11 | async-start | bytes 10616832 | tf_op jit(solution)/shard_map/reduce_scatter | solution.py:161
  828.4 207.9 %reduce-scatter.14.cloned.1.call-start = ((), (), s32[]{:S(2)}) async-start(), calls=%async_computation.12 | async-start | bytes 10616832 | tf_op jit(solution)/shard_map/reduce_scatter | solution.py:162
  844.6 228.7 %reduce-scatter.16.cloned.1.call-start = ((), (), s32[]{:S(2)}) async-start(), calls=%async_computation.13 | async-start | bytes 442368
  845.2 7.6 copy-start.10
  845.2 7.6 copy-start.11
  845.2 8.8 copy-start.43
  872.7 4.1 copy-start.25
  872.7 4.8 copy-start.3
  876.8 3.8 copy-start.36
  876.8 3.9 copy-start.41
  876.8 5.2 copy-start.23
  881.7 271.3 %all-reduce.3.cloned.1.call-start = ((), (), s32[]{:S(2)}) async-start(), calls=%async_computation.14 | async-start | bytes 3538944 | tf_op jit(solution)/shard_map/psum | solution.py:166
  (8 other events, 10.4 us)
Sparse Core Ops, SparseCore 0:
  9.9 36.6 all-gather.5
  48.5 24.0 all-gather.7
  74.5 39.7 all-gather.9
  116.0 38.9 all-gather.11
  455.6 42.4 reduce-scatter.9
  810.8 65.4 reduce-scatter.7
  879.8 76.4 reduce-scatter.11
  959.8 76.4 reduce-scatter.13
  1039.4 33.8 reduce-scatter.15
  1076.4 76.5 all-reduce.2
where the time goes:
time: 1190 us; the launch traced here: 1170 us
  matrix products  579 us (49%)
  waiting for transfers between devices  232 us (19%)
  local copies, waits for them, and re-layouts  206 us (17%)
  other arithmetic  111 us (9%)
  blocking collectives  22.2 us (2%)
  between operations  15.3 us (1%)
    dot_general x76, matrix products, against(): lax.dot_general(left, right, (((1,), (1,)), ((), ())), preferred_element_...  211 us
    dot_general x52, matrix products, product(): return jnp.dot(left, right, preferred_element_type=jnp.float32)  206 us
    dot_general x52, matrix products, outer_sum(): lax.dot_general(left, right, (((0,), (0,)), ((), ())), preferred_element_...  162 us
    reduce_scatter x1, waiting for transfers between devices, per_device(): lax.psum_scatter(grad_down, 'fsdp', scatter_dimension=1, tiled=True)  77.9 us
    psum x1, waiting for transfers between devices, per_device(): lax.psum(owned[1].astype(jnp.bfloat16), 'rep').astype(jnp.float32)  66.5 us
    reduce_scatter x1, waiting for transfers between devices, per_device(): lax.psum_scatter(grad_up, 'fsdp', scatter_dimension=1, tiled=True)  55.7 us
    reshape x4, local copies, waits for them, and re-layouts, split_heads(): shaped.transpose(0, 2, 1, 3).reshape(rows * heads, count // rows, HEAD)  39.2 us
    unnamed x104, local copies, waits for them, and re-layouts  35.3 us
  transfers between devices with their start and end apart: 10, of which 5 were waited for; matrix products, arithmetic and copies ran while one was open for 68% of the time, Pallas kernels for 0%

commit v1 on v0

--- a/solution.py
+++ b/solution.py
@@ -7,6 +7,9 @@
 ROW_LEN = 1024
 layer_eps = 1e-06
 ema_rate = 0.75
+define_the_trails = lambda view, which_axis: jnp.sum(
+    lax.all_gather(view, axis_name=which_axis), axis=0
+)
 
 
 def layer_norm(values, gain, shift):
@@ -163,7 +166,7 @@
     )
     summed = (
         lax.psum(owned[0].astype(jnp.bfloat16), "rep").astype(jnp.float32),
-        lax.psum(owned[1].astype(jnp.bfloat16), "rep").astype(jnp.float32),
+        define_the_trails(owned[1].astype(jnp.bfloat16), "rep").astype(jnp.float32),
         lax.psum(owned[2].astype(jnp.bfloat16), "rep").astype(jnp.float32),
         lax.psum(owned[3].astype(jnp.bfloat16), "rep").astype(jnp.float32),
         lax.psum(owned[4].astype(jnp.bfloat16), "rep").astype(jnp.float32),

time: 1190 us -> 1270 us (1.067)
  waiting for transfers between devices: 232 us -> 290 us
  matrix products: 579 us -> 599 us
    all_gather x0 -> x1, waiting for transfers between devices: none -> 29.1 us  [lax.all_gather(view, axis_name=which_axis)]
    reduce_scatter x1, waiting for transfers between devices: 55.7 us -> 78.4 us  [per_device(): lax.psum_scatter(grad_up, 'fsdp', scatter_dimension=1, tiled=True)]
    dot_general x52, matrix products: 206 us -> 221 us  [product(): return jnp.dot(left, right, preferred_element_type=jnp.float32)]
    unnamed x104 -> x102, local copies, waits for them, and re-layouts: 35.3 us -> 35.6 us
  transfers between devices with their start and end apart: 10 -> 11, of which waited for: 5 -> 7; matrix products, arithmetic and copies ran while one was open for 68% -> 36% of each run, Pallas kernels for 0% -> 0%
where the time goes in v1:
time: 1270 us; the launch traced here: 1250 us
  matrix products  599 us (47%)
  waiting for transfers between devices  290 us (23%)
  local copies, waits for them, and re-layouts  213 us (17%)
  other arithmetic  111 us (9%)
  blocking collectives  22.2 us (2%)
  between operations  15 us (1%)
    dot_general x52, matrix products, product(): return jnp.dot(left, right, preferred_element_type=jnp.float32)  221 us
    dot_general x76, matrix products, against(): lax.dot_general(left, right, (((1,), (1,)), ((), ())), preferred_element_...  211 us
    dot_general x52, matrix products, outer_sum(): lax.dot_general(left, right, (((0,), (0,)), ((), ())), preferred_element_...  166 us
    reduce_scatter x1, waiting for transfers between devices, per_device(): lax.psum_scatter(grad_up, 'fsdp', scatter_dimension=1, tiled=True)  78.4 us
    reduce_scatter x1, waiting for transfers between devices, per_device(): lax.psum_scatter(grad_down, 'fsdp', scatter_dimension=1, tiled=True)  77.9 us
    psum x1, waiting for transfers between devices, per_device(): lax.psum(owned[2].astype(jnp.bfloat16), 'rep').astype(jnp.float32)  56.7 us
    reshape x4, local copies, waits for them, and re-layouts, split_heads(): shaped.transpose(0, 2, 1, 3).reshape(rows * heads, count // rows, HEAD)  39.1 us
    unnamed x102, local copies, waits for them, and re-layouts  35.6 us
  transfers between devices with their start and end apart: 11, of which 7 were waited for; matrix products, arithmetic and copies ran while one was open for 36% of the time, Pallas kernels for 0%

profile of v1, /device:TPU:0, one launch (start us, length us, event | category | flops | bytes accessed | tf_op | source)
XLA Modules:
  0.0 1252.7 jit_solution(18219589154975229707)
XLA Ops:
  17.2 10.4 all-gather.1
  27.8 4.7 copy.127
  32.5 14.1 %all-gather.8.cloned.1.call-done = bf16[768,2304]{0,1:T(8,128)(2,1)} async-done(((bf16[768,288]{0,1:T(8,128)(2,1)}), bf16[768,2304]{0,1:T(8,128)(2,1)}) %all-gather.8.cloned.1.call-update) | async-done | bytes 3538960 | tf_op jit(solution)/shard_map/all_gather | solution.py:100
  46.6 10.6 convolution_convert_fusion
  57.3 3.8 fusion.77
  61.1 4.7 copy.116
  65.8 6.1 reshape.164
  71.9 9.8 copy.144
  81.7 4.7 copy.118
  86.4 6.1 reshape.166
  92.6 9.8 copy.145
  102.4 4.6 copy.120
  107.0 6.1 reshape.168
  113.1 9.7 copy.146
  124.9 153.1 %while.28 = (s32[]{:T(128)}, bf16[24,1024,64]{1,2,0:T(8,128)(2,1)}, f32[24,1024,1]{1,2,0:T(1,128)}, f32[24,1024,1]{1,2,0:T(1,128)}, s32[24,1024]{1,0:T(8,128)S(1...) while((s32[]{:T(128)}, bf16[24,1024,64]{1,2,0:T(8,128)(2,1)}, ...), condition=%wide.region_5.6_spmd, body=%wide.region_2.5_spmd.sunk | while | flops 284162048 | bytes 13699681 | solution.py:117
  278.0 5.2 copy.125
  285.9 4.9 fusion.78
  296.2 67.6 %multiply_convert_fusion.1 = (bf16[2048,3072]{1,0:T(8,128)(2,1)}, f32[2048,3072]{1,0:T(8,128)}, f32[2048,3072]{1,0:T(8,128)}) fusion(bf16[768,3072]{1,0:T(8,128)(2,1)} %all-gather.12.cloned.1.call-done, bf16[2048,768]{0,1:T(8,128)(2,1)} %add_convert_fusion.4.clone.4), kind=kOutput, calls=%fused_computation.61 | convolution fusion | flops 10072621056 | bytes 70778880 | tf_op jit(solution)/shard_map/dot_general | solution.py:26
  363.9 27.9 %add_convert_fusion = bf16[2048,3072]{1,0:T(8,128)(2,1)} fusion(f32[2048,3072]{1,0:T(8,128)} %get-tuple-element.290, f32[2048,3072]{1,0:T(8,128)} %get-tuple-element.304, bf16[3072,768]{0,1:T(8,128)(2,1)} %all-gather.14.cloned.1.call-done, bf16[2048,768]{0,1:T(8,128)(2,1)S(1)} %copy-done.6, f32[2048]{0:T(1024)S(1)} %copy-done.21), kind=kOutput, calls=%fused_computation.60 | convolution fusion | flops 9756475392 | bytes 70787072 | tf_op jit(solution)/shard_map/dot_general | solution.py:36
  391.8 16.5 %fusion.79 = (f32[768]{0:T(1024)}, f32[2048,768]{1,0:T(8,128)}) fusion(bf16[2048,3072]{1,0:T(8,128)(2,1)} %add_convert_fusion, bf16[768,3072]{1,0:T(8,128)(2,1)} %all-gather.12.cloned.1.call-done), kind=kOutput, calls=%fused_computation.135 | convolution fusion | flops 9665248256 | bytes 23596032 | tf_op jit(solution)/shard_map/dot_general | solution.py:36
  408.4 6.7 copy.128
  415.1 6.4 multiply_reduce_fusion.1
  421.5 3.9 fusion.75
  429.7 4.2 convolution_convert_fusion.1
  437.1 3.9 reshape.170
  441.1 9.7 copy.149
  457.0 336.0 %while.29 = (s32[]{:T(128)}, bf16[24,1024,64]{1,2,0:T(8,128)(2,1)}, bf16[24,1024,64]{1,2,0:T(8,128)(2,1)}, bf16[24,1024,64]{1,2,0:T(8,128)(2,1)}, s32[24,1024]{1...) while((s32[]{:T(128)}, bf16[24,1024,64]{1,2,0:T(8,128)(2,1)}, ...), condition=%wide.region_12.13_spmd, body=%wide.region_10.12_spmd.sunk | while | flops 682753024 | bytes 34133116 | solution.py:147
  793.0 5.1 copy.135
  804.3 5.3 copy.137
  811.3 3.7 copy-done.12
  815.1 10.0 fusion.70
  825.1 6.9 fusion.81
  832.1 19.3 %fusion.73 = f32[768,3072]{1,0:T(8,128)} fusion(bf16[2048,3072]{1,0:T(8,128)(2,1)} %add_convert_fusion, f32[2048,768]{0,1:T(8,128)} %copy-done.2, f32[768]{0:T(1024)S(1)} %copy-done.35, f32[768]{0:T(1024)S(1)} %copy-done.33, f32[2048]{0:T(1024)S(1)} %copy-done.20, f32[2048]{0:T(1024)S(1)} %copy-done.15), kind=kOutput, calls=%fused_computation.130 | convolution fusion | flops 9671540736 | bytes 28334080 | tf_op jit(solution)/shard_map/dot_general | solution.py:30
  851.4 16.1 %fusion.66 = f32[3072,768]{0,1:T(8,128)} fusion(bf16[2048,3072]{1,0:T(8,128)(2,1)} %get-tuple-element.289, bf16[2048,768]{0,1:T(8,128)(2,1)} %copy.127, f32[2048]{0:T(1024)S(1)} %copy-done.21), kind=kOutput, calls=%fused_computation.102 | convolution fusion | flops 9668395008 | bytes 25174016 | tf_op jit(solution)/shard_map/dot_general | solution.py:30
  876.5 12.6 %fusion.80 = (f32[768]{0:T(1024)S(1)}, f32[2048,768]{1,0:T(8,128)}) fusion(bf16[2048,2304]{0,1:T(8,128)(2,1)} %copy-done.12, bf16[768,2304]{0,1:T(8,128)(2,1)S(1)} %copy-done.43), kind=kOutput, calls=%fused_computation.136 | convolution fusion | flops 7249329152 | bytes 19270656 | tf_op jit(solution)/shard_map/dot_general | solution.py:36
  889.1 6.7 copy.138
  895.8 4.0 fusion.64
  907.6 16.6 %multiply_convert_fusion.3 = bf16[2048,768]{0,1:T(8,128)(2,1)} fusion(f32[2048,768]{0,1:T(8,128)} %copy-done.2, bf16[2048,3072]{1,0:T(8,128)(2,1)} %get-tuple-element.289, bf16[3072,768]{0,1:T(8,128)(2,1)} %all-gather.14.cloned.1.call-done, f32[2048]{0:T(1024)S(1)} %copy-done.21), kind=kOutput, calls=%fused_computation.97 | convolution fusion | flops 9668395008 | bytes 26746880 | tf_op jit(solution)/shard_map/dot_general | solution.py:26
  924.2 12.6 %reduce-scatter.10.cloned.1.call-done = f32[768,96]{0,1:T(8,128)} async-done(((f32[768,768]{0,1:T(8,128)}), f32[768,96]{0,1:T(8,128)}) %reduce-scatter.10.cloned.1.call-update) | async-done | bytes 294928 | tf_op jit(solution)/shard_map/reduce_scatter | solution.py:163
  938.4 78.4 %reduce-scatter.12.cloned.1.call-done = f32[768,384]{1,0:T(8,128)} async-done(((f32[768,3072]{1,0:T(8,128)}), f32[768,384]{1,0:T(8,128)}) %reduce-scatter.12.cloned.1.call-update) | async-done | bytes 1179664 | tf_op jit(solution)/shard_map/reduce_scatter | solution.py:164
  1019.0 77.9 %reduce-scatter.14.cloned.1.call-done = f32[3072,96]{0,1:T(8,128)} async-done(((f32[3072,768]{0,1:T(8,128)}), f32[3072,96]{0,1:T(8,128)}) %reduce-scatter.14.cloned.1.call-update) | async-done | bytes 1179664 | tf_op jit(solution)/shard_map/reduce_scatter | solution.py:165
  1099.0 8.3 add_convert_fusion.1
  1107.3 4.8 copy.142
  1114.9 18.8 %reduce-scatter.16.cloned.1.call-done = f32[96,4]{1,0:T(8,128)} async-done(((f32[768,4]{1,0:T(8,128)}), f32[96,4]{1,0:T(8,128)}) %reduce-scatter.16.cloned.1.call-update) | async-done | bytes 1552
  1134.6 11.8 psum.28
  1147.0 29.1 %all-gather.16.cloned.1.call-done = bf16[3072,288]{0,1:T(8,128)(2,1)} async-done(((bf16[768,288]{0,1:T(8,128)(2,1)}), bf16[3072,288]{0,1:T(8,128)(2,1)}) %all-gather.16.cloned.1.call-update) | async-done | bytes 1769488 | tf_op jit(solution)/shard_map/all_gather | solution.py:11
  1176.1 3.5 reshape.182
  1183.0 56.7 %all-reduce.3.cloned.1.call-done = (bf16[768,96]{0,1:T(8,128)(2,1)}, bf16[768,384]{1,0:T(8,128)(2,1)}, bf16[3072,96]{0,1:T(8,128)(2,1)}) async-done(((bf16[768,96]{0,1:T(8,128)(2,1)}, bf16[768,384]{1,0:T(8,128)(2,1)}, bf16[3072,96]{0,1:T(8,128)(2,1)}), (bf16[768,96]{0,1:T(8,128)(2,1)}, bf16[768,384]{1,0:T(8,128)(2,1)}, bf16[3072,96]{0,1:T(8,128)(2,1)})) %all-reduce.3.cloned.1.call-update) | async-done | bytes 1327120 | tf_op jit(solution)/shard_map/psum | solution.py:170
  (487 shorter events, 565.6 us)
Async XLA Ops:
  7.2 39.4 %all-gather.8.cloned.1.call-start = ((), (), s32[]{:S(2)}) async-start(), calls=%async_computation.5 | async-start | bytes 3981312 | tf_op jit(solution)/shard_map/all_gather | solution.py:100
  7.9 278.0 %all-gather.10.cloned.1.call-start = ((), (), s32[]{:S(2)}) async-start(), calls=%async_computation.6 | async-start | bytes 1327104 | tf_op jit(solution)/shard_map/all_gather | solution.py:101
  8.7 287.6 %all-gather.12.cloned.1.call-start = ((), (), s32[]{:S(2)}) async-start(), calls=%async_computation.7 | async-start | bytes 5308416 | tf_op jit(solution)/shard_map/all_gather | solution.py:102
  9.4 354.5 %all-gather.14.cloned.1.call-start = ((), (), s32[]{:S(2)}) async-start(), calls=%async_computation.8 | async-start | bytes 5308416 | tf_op jit(solution)/shard_map/all_gather | solution.py:103
  10.0 895.5 %reduce-scatter.8.cloned.1.call-start = ((), (), s32[]{:S(2)}) async-start(), calls=%async_computation.9 | async-start | bytes 7962624 | tf_op jit(solution)/shard_map/reduce_scatter | solution.py:162
  12.0 5.2 copy-start.39
  15.2 270.6 %copy-start = (bf16[2048,768]{0,1:T(8,128)(2,1)}, bf16[2048,768]{0,1:T(8,128)(2,1)S(1)}, u32[]{:S(2)}) copy-start(bf16[2048,768]{0,1:T(8,128)(2,1)S(1)} %copy.114) | copy-start | bytes 9437188
  15.8 41.5 %copy-start.16 = (f32[2048]{0:T(1024)}, f32[2048]{0:T(1024)S(1)}, u32[]{:S(2)}) copy-start(f32[2048]{0:T(1024)S(1)} %broadcast_multiply_fusion.1) | copy-start | bytes 24580
  17.2 40.0 %copy-start.28 = (f32[2048]{0:T(1024)}, f32[2048]{0:T(1024)S(1)}, u32[]{:S(2)}) copy-start(f32[2048]{0:T(1024)S(1)} %fusion.68) | copy-start | bytes 24580
  27.7 29.5 %copy-start.30 = (f32[768]{0:T(1024)}, f32[768]{0:T(1024)S(1)}, u32[]{:S(2)}) copy-start(f32[768]{0:T(1024)S(1)} %get-tuple-element.245) | copy-start | bytes 9220
  27.7 29.5 %copy-start.37 = (f32[768]{0:T(1024)}, f32[768]{0:T(1024)S(1)}, u32[]{:S(2)}) copy-start(f32[768]{0:T(1024)S(1)} %get-tuple-element.244) | copy-start | bytes 9220
  27.8 263.8 %copy-start.32 = (f32[768]{0:T(1024)}, f32[768]{0:T(1024)S(1)}, u32[]{:S(2)}) copy-start(f32[768]{0:T(1024)S(1)} %get-tuple-element.242) | copy-start | bytes 9220
  27.8 263.8 %copy-start.34 = (f32[768]{0:T(1024)}, f32[768]{0:T(1024)S(1)}, u32[]{:S(2)}) copy-start(f32[768]{0:T(1024)S(1)} %get-tuple-element.243) | copy-start | bytes 9220
  278.0 7.9 copy-start.18
  290.8 5.4 copy-start.14
  291.5 4.7 copy-start.26
  291.5 4.7 copy-start.19
  296.2 67.7 %copy-start.6 = (bf16[2048,768]{0,1:T(8,128)(2,1)S(1)}, bf16[2048,768]{0,1:T(8,128)(2,1)}, u32[]{:S(2)}) copy-start(bf16[2048,768]{0,1:T(8,128)(2,1)} %copy.127) | copy-start | bytes 9437188
  296.2 67.7 %copy-start.21 = (f32[2048]{0:T(1024)S(1)}, f32[2048]{0:T(1024)}, u32[]{:S(2)}) copy-start(f32[2048]{0:T(1024)} %compare_convert_fusion) | copy-start | bytes 24580
  408.4 6.7 copy-start.15
  408.4 6.7 copy-start.20
  408.4 6.7 copy-start.33
  415.0 6.4 copy-start.27
  415.0 6.4 copy-start.4
  425.4 4.3 copy-start.44
  810.6 4.4 copy-start.1
  810.6 4.4 copy-start.17
  810.7 4.4 copy-start.29
  810.7 4.4 copy-start.31
  810.7 4.4 copy-start.38
  825.1 7.0 copy-start.35
  825.1 111.7 %reduce-scatter.10.cloned.1.call-start = ((), (), s32[]{:S(2)}) async-start(), calls=%async_computation.10 | async-start | bytes 2654208 | tf_op jit(solution)/shard_map/reduce_scatter | solution.py:163
  832.0 184.8 %reduce-scatter.12.cloned.1.call-start = ((), (), s32[]{:S(2)}) async-start(), calls=%async_computation.11 | async-start | bytes 10616832 | tf_op jit(solution)/shard_map/reduce_scatter | solution.py:164
  851.4 245.4 %reduce-scatter.14.cloned.1.call-start = ((), (), s32[]{:S(2)}) async-start(), calls=%async_computation.12 | async-start | bytes 10616832 | tf_op jit(solution)/shard_map/reduce_scatter | solution.py:165
  867.6 266.1 %reduce-scatter.16.cloned.1.call-start = ((), (), s32[]{:S(2)}) async-start(), calls=%async_computation.14 | async-start | bytes 442368
  868.5 6.8 copy-start.10
  868.5 6.8 copy-start.11
  868.5 8.0 copy-start.43
  895.8 4.0 copy-start.25
  895.8 4.8 copy-start.3
  899.8 4.0 copy-start.36
  899.8 4.0 copy-start.41
  899.8 5.1 copy-start.40
  899.9 5.1 copy-start.42
  904.8 271.2 %all-gather.16.cloned.1.call-start = ((), (), s32[]{:S(2)}) async-start(), calls=%async_computation.13 | async-start | bytes 2211840 | tf_op jit(solution)/shard_map/all_gather | solution.py:11
  907.5 191.5 %copy-start.23 = (f32[2048]{0:T(1024)S(1)}, f32[2048]{0:T(1024)}, u32[]{:S(2)}) copy-start(f32[2048]{0:T(1024)} %copy-done.22) | copy-start | bytes 24580
  907.5 332.2 %all-reduce.3.cloned.1.call-start = ((), (), s32[]{:S(2)}) async-start(), calls=%async_computation.15 | async-start | bytes 2654208 | tf_op jit(solution)/shard_map/psum | solution.py:170
  1107.3 4.8 copy-start.8
  (8 other events, 16.9 us)
Sparse Core Ops, SparseCore 0:
  9.9 36.6 all-gather.7
  48.5 24.0 all-gather.9
  74.5 39.7 all-gather.11
  116.0 38.9 all-gather.13
  825.2 65.4 reduce-scatter.7
  894.3 42.4 reduce-scatter.9
  940.3 76.4 reduce-scatter.11
  1020.3 76.4 reduce-scatter.13
  1099.9 33.8 reduce-scatter.15
  1135.7 40.2 all-gather.15
  1179.2 60.4 all-reduce.2
